TPU v7x, 32 devices: a whole 2x2x4 slice. The times are simulated.
32 devices in a mesh: dp: 8 (over z, x), tensor: 4 (over y, core).
Axes of the slice: x: 2, y: 2, z: 4, core: 2. Of those that a mesh axis runs over, the one named last changes fastest.
Arguments:
- tokens: bfloat16 [8192, 1024], P('dp')
- segments: int32 [8, 1024], P('dp'), may hold values from -1 to 16, as said below
- w_query: bfloat16 [1024, 1024], P(None, 'tensor'), may hold values from -0.1875 to 0.1875
- w_key: bfloat16 [1024, 1024], P(None, 'tensor'), may hold values from -0.1875 to 0.1875
- w_value: bfloat16 [1024, 1024], P(None, 'tensor'), may hold values from -0.1875 to 0.1875
- w_out: bfloat16 [1024, 1024], P(None, 'tensor'), may hold values from -0.1875 to 0.1875
- w_fc1: bfloat16 [1024, 4096], P(None, 'tensor'), may hold values from -0.1875 to 0.1875
- w_fc2: bfloat16 [1024, 4096], P(None, 'tensor'), may hold values from -0.09375 to 0.09375
- ln1_gain: float32 [1024], replicated, may hold values from 0.5 to 1.5
- ln1_bias: float32 [1024], replicated, may hold values from -1.2 to 1.2
- post_gain: float32 [1024], replicated, may hold values from 0.5 to 1.5
- post_bias: float32 [1024], replicated, may hold values from -1.2 to 1.2
- ln2_gain: float32 [1024], replicated, may hold values from 0.5 to 1.5
- ln2_bias: float32 [1024], replicated, may hold values from -1.2 to 1.2
- mid_gain: float32 [4096], P('tensor'), may hold values from 0.5 to 1.5
- mid_bias: float32 [4096], P('tensor'), may hold values from -1.2 to 1.2
- query_bias: float32 [1024], P('tensor'), may hold values from -1.2 to 1.2
- value_bias: float32 [1024], P('tensor'), may hold values from -1.2 to 1.2
- out_bias: float32 [1024], replicated, may hold values from -1.2 to 1.2
- fc1_bias: float32 [4096], P('tensor'), may hold values from -1.2 to 1.2
- fc2_bias: float32 [1024], replicated, may hold values from -1.2 to 1.2
- head_scale: float32 [16], P('tensor'), may hold values from 0.25 to 1.75
- cotangent: bfloat16 [8192, 1024], P('dp'), may hold values from -6 to 6
Outputs:
- output: bfloat16 [8192, 1024], P('dp')
- grad_tokens: float32 [8192, 1024], P('dp')
- grad_w_query: float32 [1024, 1024], P('dp', 'tensor')
- grad_w_key: float32 [1024, 1024], P('dp', 'tensor')
- grad_w_value: float32 [1024, 1024], P('dp', 'tensor')
- grad_w_out: float32 [1024, 1024], P('dp', 'tensor')
- grad_w_fc1: float32 [1024, 4096], P('dp', 'tensor')
- grad_w_fc2: float32 [1024, 4096], P('dp', 'tensor')
- grad_ln1_gain: float32 [1024], replicated
- grad_ln1_bias: float32 [1024], replicated
- grad_post_gain: float32 [1024], replicated
- grad_post_bias: float32 [1024], replicated
- grad_ln2_gain: float32 [1024], replicated
- grad_ln2_bias: float32 [1024], replicated
- grad_mid_gain: float32 [4096], P('tensor')
- grad_mid_bias: float32 [4096], P('tensor')
- grad_query_bias: float32 [1024], P('tensor')
- grad_value_bias: float32 [1024], P('tensor')
- grad_out_bias: float32 [1024], replicated
- grad_fc1_bias: float32 [4096], P('tensor')
- grad_fc2_bias: float32 [1024], replicated
- grad_head_scale: float32 [16], P('tensor')
- rms: float32 [3], replicated
Inputs may be any that keep to these rules, and one draw needn't show every extreme that they name: `segments`: each row of 1024 tokens holds whole documents of 60 to 800 tokens, numbered 0, 1, 2 and so on from the row's start, then padding marked -1 where the next document would not fit; the first document always fits. Some row holds only documents of 60 tokens followed by padding.
All inputs are finite; a program needn't handle non-finite values.
Results may differ from a plain program's by a relative error of at most 0.014.
Values sent between devices are 32-bit elements; how exact they have to be, the bound alone decides.
No kernel may reach another device: no remote copies, remote signals or barrier semaphores. Data moves between devices by JAX's collectives and lax.ppermute only.
A program may use at most 128 MiB of HBM per device.

v0:
```python
import jax
import jax.numpy as jnp
from jax import lax
from jax.sharding import PartitionSpec as P

D = 1024
HEAD_DIM = 64
FF = 4096
epsilon = 1e-05


def normalize(v):
    mean = jnp.mean(v, axis=-1, keepdims=True)
    centred = v - mean
    factor = lax.rsqrt(jnp.mean(centred * centred, axis=-1, keepdims=True) + epsilon)
    return (centred * factor, factor)


def norm_back(scaled, normed, factor):
    return factor * (
        scaled
        - jnp.mean(scaled, axis=-1, keepdims=True)
        - normed * jnp.mean(scaled * normed, axis=-1, keepdims=True)
    )


def project(left, right):
    return jnp.dot(left, right, preferred_element_type=jnp.float32)


def project_t(left, right):
    return lax.dot_general(
        left, right, (((1,), (1,)), ((), ())), preferred_element_type=jnp.float32
    )


def outer_sum(left, right):
    return lax.dot_general(
        left, right, (((0,), (0,)), ((), ())), preferred_element_type=jnp.float32
    )


def gelu_tanh(v):
    return jax.nn.gelu(v, approximate=True)


def block_scores(query_rows, keys, seg_rows, seg_keys, first):
    scores = jnp.einsum(
        "qhd,khd->hqk", query_rows, keys, preferred_element_type=jnp.float32
    ) * HEAD_DIM ** (-0.5)
    places = first + jnp.arange(query_rows.shape[0])
    allowed = (seg_rows[:, None] == seg_keys[None, :]) & (
        jnp.arange(keys.shape[0])[None, :] <= places[:, None]
    )
    return jnp.where(allowed[None], scores, -1e30)


def attend(query4, key4, value4, segments, block):
    length = query4.shape[1]
    count = length // block

    def per_sequence(item):
        queries, keys, values, seg = item

        def per_block(index):
            first = index * block
            rows_q = lax.dynamic_slice_in_dim(queries, first, block, 0)
            rows_seg = lax.dynamic_slice_in_dim(seg, first, block, 0)
            scores = block_scores(rows_q, keys, rows_seg, seg, first)
            top = jnp.max(scores, axis=-1, keepdims=True)
            expo = jnp.exp(scores - top)
            total = jnp.sum(expo, axis=-1, keepdims=True)
            weights = (expo / total).astype(jnp.bfloat16)
            result = jnp.einsum("hqk,khd->qhd", weights, values, preferred_element_type=jnp.float32)
            return (result, (top + jnp.log(total))[..., 0])

        results, logsum = lax.map(per_block, jnp.arange(count))
        return (results.reshape(length, results.shape[2], results.shape[3]), logsum)

    return lax.map(per_sequence, (query4, key4, value4, segments))


def attend_back(query4, key4, value4, segments, logsum, grad4, block):
    length = query4.shape[1]
    count = length // block
    factor = HEAD_DIM ** (-0.5)

    def per_sequence(item):
        queries, keys, values, seg, seq_logsum, grads = item

        def per_block(carry, index):
            key_grad, value_grad = carry
            first = index * block
            rows_q = lax.dynamic_slice_in_dim(queries, first, block, 0)
            rows_seg = lax.dynamic_slice_in_dim(seg, first, block, 0)
            rows_grad = lax.dynamic_slice_in_dim(grads, first, block, 0)
            scores = block_scores(rows_q, keys, rows_seg, seg, first)
            probs = jnp.exp(scores - seq_logsum[index][..., None])
            weights = probs.astype(jnp.bfloat16)
            value_grad = value_grad + jnp.einsum(
                "hqk,qhd->khd", weights, rows_grad, preferred_element_type=jnp.float32
            )
            prob_grad = jnp.einsum(
                "qhd,khd->hqk", rows_grad, values, preferred_element_type=jnp.float32
            )
            along = jnp.sum(probs * prob_grad, axis=-1, keepdims=True)
            score_grad = (probs * (prob_grad - along)).astype(jnp.bfloat16)
            query_grad = (
                jnp.einsum("hqk,khd->qhd", score_grad, keys, preferred_element_type=jnp.float32)
                * factor
            )
            key_grad = (
                key_grad
                + jnp.einsum("hqk,qhd->khd", score_grad, rows_q, preferred_element_type=jnp.float32)
                * factor
            )
            return ((key_grad, value_grad), query_grad)

        zeros = jnp.zeros(keys.shape, jnp.float32)
        (key_grad, value_grad), query_grad = lax.scan(per_block, (zeros, zeros), jnp.arange(count))
        return (query_grad.reshape(length, keys.shape[1], keys.shape[2]), key_grad, value_grad)

    return lax.map(per_sequence, (query4, key4, value4, segments, logsum, grad4))


def body(
    tokens,
    segments,
    w_query,
    w_key,
    w_value,
    w_out,
    w_fc1,
    w_fc2,
    ln1_gain,
    ln1_bias,
    post_gain,
    post_bias,
    ln2_gain,
    ln2_bias,
    mid_gain,
    mid_bias,
    query_bias,
    value_bias,
    out_bias,
    fc1_bias,
    fc2_bias,
    head_scale,
    cotangent,
):
    rows = tokens.shape[0]
    seqs = segments.shape[0]
    length = segments.shape[1]
    block = min(512, length)
    heads = w_query.shape[1] // HEAD_DIM
    shape4 = (seqs, length, heads, HEAD_DIM)
    resid = tokens.astype(jnp.float32)
    normed1, factor1 = normalize(resid)
    entry = (normed1 * ln1_gain + ln1_bias).astype(jnp.bfloat16)
    query = (project(entry, w_query) + query_bias).astype(jnp.bfloat16)
    keyed = project(entry, w_key).astype(jnp.bfloat16)
    valued = (project(entry, w_value) + value_bias).astype(jnp.bfloat16)
    query4 = query.reshape(shape4)
    key4 = keyed.reshape(shape4)
    value4 = valued.reshape(shape4)
    attended, logsum = attend(query4, key4, value4, segments, block)
    attended = attended.reshape(rows, heads, HEAD_DIM)
    context = (attended * head_scale[:, None]).reshape(rows, heads * HEAD_DIM).astype(jnp.bfloat16)
    mixed = lax.psum(project_t(context, w_out), "tensor") + out_bias
    normedp, factorp = normalize(mixed)
    branch = normedp * post_gain + post_bias
    stream = resid + branch
    normed2, factor2 = normalize(stream)
    inner = (normed2 * ln2_gain + ln2_bias).astype(jnp.bfloat16)
    hidden = project(inner, w_fc1) + fc1_bias
    active, gelu_pull = jax.vjp(gelu_tanh, hidden)
    mean = lax.psum(jnp.sum(active, axis=-1, keepdims=True), "tensor") / FF
    centred = active - mean
    spread = lax.psum(jnp.sum(centred * centred, axis=-1, keepdims=True), "tensor") / FF
    factorm = lax.rsqrt(spread + epsilon)
    normedm = centred * factorm
    middle = (normedm * mid_gain + mid_bias).astype(jnp.bfloat16)
    ffn_out = lax.psum(project_t(middle, w_fc2), "tensor") + fc2_bias
    result = stream + ffn_out
    output = result.astype(jnp.bfloat16)
    upstream = cotangent.astype(jnp.float32)
    grad_fc2_bias = jnp.sum(upstream, axis=0)
    grad_w_fc2 = outer_sum(cotangent, middle)
    grad_middle = project(cotangent, w_fc2)
    grad_mid_gain = jnp.sum(grad_middle * normedm, axis=0)
    grad_mid_bias = jnp.sum(grad_middle, axis=0)
    scaled = grad_middle * mid_gain
    sum_plain, sum_normed = lax.psum(
        (
            jnp.sum(scaled, axis=-1, keepdims=True),
            jnp.sum(scaled * normedm, axis=-1, keepdims=True),
        ),
        "tensor",
    )
    grad_active = factorm * (scaled - sum_plain / FF - normedm * (sum_normed / FF))
    grad_hidden = gelu_pull(grad_active)[0].astype(jnp.bfloat16)
    grad_fc1_bias = jnp.sum(grad_hidden.astype(jnp.float32), axis=0)
    grad_w_fc1 = outer_sum(inner, grad_hidden)
    grad_inner = lax.psum(project_t(grad_hidden, w_fc1), "tensor")
    grad_ln2_gain = jnp.sum(grad_inner * normed2, axis=0)
    grad_ln2_bias = jnp.sum(grad_inner, axis=0)
    grad_stream = upstream + norm_back(grad_inner * ln2_gain, normed2, factor2)
    grad_post_gain = jnp.sum(grad_stream * normedp, axis=0)
    grad_post_bias = jnp.sum(grad_stream, axis=0)
    grad_mixed = norm_back(grad_stream * post_gain, normedp, factorp).astype(jnp.bfloat16)
    grad_out_bias = jnp.sum(grad_mixed.astype(jnp.float32), axis=0)
    grad_w_out = outer_sum(grad_mixed, context)
    grad_context = project(grad_mixed, w_out).reshape(rows, heads, HEAD_DIM)
    grad_head = jnp.sum(grad_context * attended, axis=(0, 2))
    grad_attended = (grad_context * head_scale[:, None]).astype(jnp.bfloat16)
    grad_q4, grad_k4, grad_v4 = attend_back(
        query4, key4, value4, segments, logsum, grad_attended.reshape(shape4), block
    )
    grad_query = grad_q4.reshape(rows, heads * HEAD_DIM).astype(jnp.bfloat16)
    grad_key = grad_k4.reshape(rows, heads * HEAD_DIM).astype(jnp.bfloat16)
    grad_value = grad_v4.reshape(rows, heads * HEAD_DIM).astype(jnp.bfloat16)
    grad_query_bias = jnp.sum(grad_query.astype(jnp.float32), axis=0)
    grad_value_bias = jnp.sum(grad_value.astype(jnp.float32), axis=0)
    grad_w_query = outer_sum(entry, grad_query)
    grad_w_key = outer_sum(entry, grad_key)
    grad_w_value = outer_sum(entry, grad_value)
    grad_entry = lax.psum(
        project_t(grad_query, w_query)
        + project_t(grad_key, w_key)
        + project_t(grad_value, w_value),
        "tensor",
    )
    grad_ln1_gain = jnp.sum(grad_entry * normed1, axis=0)
    grad_ln1_bias = jnp.sum(grad_entry, axis=0)
    grad_tokens = grad_stream + norm_back(grad_entry * ln1_gain, normed1, factor1)
    valid = (segments >= 0).reshape(rows, 1).astype(jnp.float32)
    squares = jnp.stack(
        [
            jnp.sum(valid * branch * branch),
            jnp.sum(valid * ffn_out * ffn_out),
            jnp.sum(valid * result * result),
        ]
    )
    counted = jnp.sum(valid)
    (
        grad_ln1_gain,
        grad_ln1_bias,
        grad_post_gain,
        grad_post_bias,
        grad_ln2_gain,
        grad_ln2_bias,
        grad_mid_gain,
        grad_mid_bias,
        grad_query_bias,
        grad_value_bias,
        grad_out_bias,
        grad_fc1_bias,
        grad_fc2_bias,
        grad_head,
        squares,
        counted,
    ) = lax.psum(
        (
            grad_ln1_gain,
            grad_ln1_bias,
            grad_post_gain,
            grad_post_bias,
            grad_ln2_gain,
            grad_ln2_bias,
            grad_mid_gain,
            grad_mid_bias,
            grad_query_bias,
            grad_value_bias,
            grad_out_bias,
            grad_fc1_bias,
            grad_fc2_bias,
            grad_head,
            squares,
            counted,
        ),
        "dp",
    )
    rms = jnp.sqrt(squares / (counted * D))
    grad_w_query, grad_w_key, grad_w_value, grad_w_out, grad_w_fc1, grad_w_fc2 = (
        lax.psum_scatter(grad_w_query, "dp", scatter_dimension=0, tiled=True),
        lax.psum_scatter(grad_w_key, "dp", scatter_dimension=0, tiled=True),
        lax.psum_scatter(grad_w_value, "dp", scatter_dimension=0, tiled=True),
        lax.psum_scatter(grad_w_out, "dp", scatter_dimension=0, tiled=True),
        lax.psum_scatter(grad_w_fc1, "dp", scatter_dimension=0, tiled=True),
        lax.psum_scatter(grad_w_fc2, "dp", scatter_dimension=0, tiled=True),
    )
    return (
        output,
        grad_tokens,
        grad_w_query,
        grad_w_key,
        grad_w_value,
        grad_w_out,
        grad_w_fc1,
        grad_w_fc2,
        grad_ln1_gain,
        grad_ln1_bias,
        grad_post_gain,
        grad_post_bias,
        grad_ln2_gain,
        grad_ln2_bias,
        grad_mid_gain,
        grad_mid_bias,
        grad_query_bias,
        grad_value_bias,
        grad_out_bias,
        grad_fc1_bias,
        grad_fc2_bias,
        grad_head,
        rms,
    )


def solution(mesh):
    return jax.shard_map(
        body,
        mesh=mesh,
        in_specs=(
            P("dp", None),
            P("dp", None),
            P(None, "tensor"),
            P(None, "tensor"),
            P(None, "tensor"),
            P(None, "tensor"),
            P(None, "tensor"),
            P(None, "tensor"),
            P(),
            P(),
            P(),
            P(),
            P(),
            P(),
            P("tensor"),
            P("tensor"),
            P("tensor"),
            P("tensor"),
            P(),
            P("tensor"),
            P(),
            P("tensor"),
            P("dp", None),
        ),
        out_specs=(
            P("dp", None),
            P("dp", None),
            P("dp", "tensor"),
            P("dp", "tensor"),
            P("dp", "tensor"),
            P("dp", "tensor"),
            P("dp", "tensor"),
            P("dp", "tensor"),
            P(),
            P(),
            P(),
            P(),
            P(),
            P(),
            P("tensor"),
            P("tensor"),
            P("tensor"),
            P("tensor"),
            P(),
            P("tensor"),
            P(),
            P("tensor"),
            P(),
        ),
        check_vma=False,
    )
```

profile of v0, /device:TPU:0, one launch (start us, length us, event | category | flops | bytes accessed | tf_op | source)
XLA Modules:
  0.0 981.3 jit_solution(746196354005105888)
XLA Ops:
  17.5 42.9 %while.47 = (s32[]{:T(128)}, f32[2,512,4,64]{1,0,3,2:T(2,128)}, f32[2,4,512]{2,1,0:T(4,128)S(1)}, s32[2]{0:T(128)S(1)}, s32[1024]{0:T(1024)S(1)}, /*index=5*/bf1...) while((s32[]{:T(128)}, f32[2,512,4,64]{1,0,3,2:T(2,128)}, ...), condition=%wide.region_5.6_spmd, body=%wide.region_2.5_spmd.sunk | while | flops 563608064 | bytes 31275212 | solution.py:77
  28.6 10.4 %dynamic_update_slice.30 = f32[2,512,4,64]{1,0,3,2:T(2,128)} dynamic-update-slice(f32[2,512,4,64]{1,0,3,2:T(2,128)} %get-tuple-element.525, f32[1,512,4,64]{1,0,3,2:T(1,128)S(1)} %copy.100, s32[]{:T(128)S(6)} %copy.107, s32[]{:T(128)} %constant.111.clone.1..sunk, s32[]{:T(128)} %constant.111.clone.1..sunk, s32[]{:T(128)} %constant.111.clone.1..sunk) | dynamic-update-slice | bytes 1048580 | tf_op jit(solution)/shard_map/while/body/eval_jaxpr/while/body/jit(dynamic_update_index_in_dim)/dynamic_update_slice | solution.py:77
  50.0 10.4 %dynamic_update_slice.30 = f32[2,512,4,64]{1,0,3,2:T(2,128)} dynamic-update-slice(f32[2,512,4,64]{1,0,3,2:T(2,128)} %get-tuple-element.525, f32[1,512,4,64]{1,0,3,2:T(1,128)S(1)} %copy.100, s32[]{:T(128)S(6)} %copy.107, s32[]{:T(128)} %constant.111.clone.1..sunk, s32[]{:T(128)} %constant.111.clone.1..sunk, s32[]{:T(128)} %constant.111.clone.1..sunk) | dynamic-update-slice | bytes 1048580 | tf_op jit(solution)/shard_map/while/body/eval_jaxpr/while/body/jit(dynamic_update_index_in_dim)/dynamic_update_slice | solution.py:77
  67.1 6.4 fusion.73
  78.9 76.3 %all-reduce.7.cloned.1.call-done = f32[1024,1024]{1,0:T(8,128)} async-done(((f32[1024,1024]{1,0:T(8,128)}), f32[1024,1024]{1,0:T(8,128)}) %all-reduce.7.cloned.1.call-update) | async-done | bytes 4194320 | tf_op jit(solution)/shard_map/psum | solution.py:169
  179.4 6.1 psum.170
  185.5 8.0 fusion.67
  197.2 6.1 all-reduce.1
  203.4 8.0 convert_reduce_fusion.2
  216.1 153.8 %all-reduce.11.cloned.1.call-done = (f32[1024,1024]{1,0:T(8,128)}, f32[1024,1024]{1,0:T(8,128)}) async-done(((f32[1024,1024]{1,0:T(8,128)}, f32[1024,1024]{1,0:T(8,128)}), (f32[1024,1024]{1,0:T(8,128)}, f32[1024,1024]{1,0:T(8,128)})) %all-reduce.11.cloned.1.call-update) | async-done | bytes 8388624 | tf_op jit(solution)/shard_map/psum | solution.py:183
  370.0 8.2 fusion.59
  379.6 6.3 multiply_reduce_fusion.3
  390.2 38.5 %while.48 = (s32[]{:T(128)}, f32[1024,4,64]{0,2,1:T(8,128)S(1)}, f32[1024,4,64]{0,2,1:T(8,128)}, bf16[2,512,4,64]{1,3,2,0:T(8,128)(2,1)S(1)}, s32[2]{0:T(128)S(1...) while((s32[]{:T(128)}, f32[1024,4,64]{0,2,1:T(8,128)S(1)}, ...), condition=%wide.region_27.28_spmd.clone, body=%wide.region_25.27_spmd.clone.sunk | while | flops 1376647680 | bytes 80812376 | solution.py:120
  436.6 7.9 convolution_bitcast_fusion
  456.2 7.6 fusion.68
  467.4 53.4 %all-reduce.9.cloned.1.call-done = f32[1024,1024]{1,0:T(8,128)} async-done(((f32[1024,1024]{1,0:T(8,128)}), f32[1024,1024]{1,0:T(8,128)}) %all-reduce.9.cloned.1.call-update) | async-done | bytes 4194320 | tf_op jit(solution)/shard_map/psum | solution.py:227
  524.6 40.9 %all-reduce = (f32[1024]{0:T(1024)}, f32[1024]{0:T(1024)}, f32[1024]{0:T(1024)}, f32[1024]{0:T(1024)}, f32[1024]{0:T(1024)}, /*index=5*/f32[1024]{0:T(1024)}, f3...) all-reduce(f32[1024]{0:T(1024)S(1)} %get-tuple-element.292, ...), channel_id=1, replica_groups=mesh['dp'=8,'tensor'=4] {'dp'}, use_global_device_ids=true, to_apply=%region_38.39 | all-reduce | flops 11784 | bytes 94272 | tf_op jit(solution)/shard_map/psum | solution.py:262
  566.6 6.4 fusion.48
  573.1 40.9 %reduce-scatter.17.cloned.1.call-done = f32[128,1024]{0,1:T(8,128)} async-done(((f32[1024,1024]{0,1:T(8,128)}), f32[128,1024]{0,1:T(8,128)}) %reduce-scatter.17.cloned.1.call-update) | async-done | bytes 524304 | tf_op jit(solution)/shard_map/reduce_scatter | solution.py:290
  616.0 65.7 %reduce-scatter.13.cloned.1.call-done = f32[128,256]{1,0:T(8,128)} async-done(((f32[1024,256]{1,0:T(8,128)}), f32[128,256]{1,0:T(8,128)}) %reduce-scatter.13.cloned.1.call-update) | async-done | bytes 131088 | tf_op jit(solution)/shard_map/reduce_scatter | solution.py:288
  681.7 67.0 %reduce-scatter.11.cloned.1.call-done = f32[128,256]{1,0:T(8,128)} async-done(((f32[1024,256]{1,0:T(8,128)}), f32[128,256]{1,0:T(8,128)}) %reduce-scatter.11.cloned.1.call-update) | async-done | bytes 131088 | tf_op jit(solution)/shard_map/reduce_scatter | solution.py:287
  748.7 67.1 %reduce-scatter.9.cloned.1.call-done = f32[128,256]{1,0:T(8,128)} async-done(((f32[1024,256]{1,0:T(8,128)}), f32[128,256]{1,0:T(8,128)}) %reduce-scatter.9.cloned.1.call-update) | async-done | bytes 131088 | tf_op jit(solution)/shard_map/reduce_scatter | solution.py:286
  815.8 67.1 %reduce-scatter.7.cloned.1.call-done = f32[128,256]{1,0:T(8,128)} async-done(((f32[1024,256]{1,0:T(8,128)}), f32[128,256]{1,0:T(8,128)}) %reduce-scatter.7.cloned.1.call-update) | async-done | bytes 131088 | tf_op jit(solution)/shard_map/reduce_scatter | solution.py:285
  882.9 91.5 %reduce-scatter.15.cloned.1.call-done = f32[128,1024]{1,0:T(8,128)} async-done(((f32[1024,1024]{1,0:T(8,128)}), f32[128,1024]{1,0:T(8,128)}) %reduce-scatter.15.cloned.1.call-update) | async-done | bytes 524304 | tf_op jit(solution)/shard_map/reduce_scatter | solution.py:289
  (267 shorter events, 143.0 us)
Async XLA Ops:
  7.2 59.9 %copy-start = (bf16[1024,1024]{1,0:T(8,128)(2,1)S(1)}, bf16[1024,1024]{1,0:T(8,128)(2,1)}, u32[]{:S(2)}) copy-start(bf16[1024,1024]{1,0:T(8,128)(2,1)} %param.34) | copy-start | bytes 6291460
  7.2 148.0 %all-reduce.7.cloned.1.call-start = ((), (), s32[]{:S(2)}) async-start(), calls=%async_computation.6 | async-start | bytes 8388608 | tf_op jit(solution)/shard_map/psum | solution.py:169
  66.8 303.1 %all-reduce.11.cloned.1.call-start = ((), (), s32[]{:S(2)}) async-start(), calls=%async_computation.14 | async-start | bytes 16777216 | tf_op jit(solution)/shard_map/psum | solution.py:183
  73.5 81.7 %copy-start.42 = (f32[1024]{0:T(1024)S(1)}, f32[1024]{0:T(1024)}, u32[]{:S(2)}) copy-start(f32[1024]{0:T(1024)} %param.45) | copy-start | bytes 12292
  78.9 80.5 %copy-start.48 = (f32[1024]{0:T(1024)S(1)}, f32[1024]{0:T(1024)}, u32[]{:S(2)}) copy-start(f32[1024]{0:T(1024)} %param.37) | copy-start | bytes 12292
  78.9 80.5 %copy-start.54 = (f32[1024]{0:T(1024)S(1)}, f32[1024]{0:T(1024)}, u32[]{:S(2)}) copy-start(f32[1024]{0:T(1024)} %param.38) | copy-start | bytes 12292
  215.8 154.1 %copy-start.58 = (f32[1024]{0:T(1024)S(1)}, f32[1024]{0:T(1024)}, u32[]{:S(2)}) copy-start(f32[1024]{0:T(1024)} %param.47) | copy-start | bytes 12292
  215.9 304.9 %all-reduce.9.cloned.1.call-start = ((), (), s32[]{:S(2)}) async-start(), calls=%async_computation.7 | async-start | bytes 8388608 | tf_op jit(solution)/shard_map/psum | solution.py:227
  435.0 179.0 %reduce-scatter.17.cloned.1.call-start = ((), (), s32[]{:S(2)}) async-start(), calls=%async_computation.13 | async-start | bytes 4718592 | tf_op jit(solution)/shard_map/reduce_scatter | solution.py:290
  444.5 237.1 %reduce-scatter.13.cloned.1.call-start = ((), (), s32[]{:S(2)}) async-start(), calls=%async_computation.11 | async-start | bytes 1179648 | tf_op jit(solution)/shard_map/reduce_scatter | solution.py:288
  449.2 299.4 %reduce-scatter.11.cloned.1.call-start = ((), (), s32[]{:S(2)}) async-start(), calls=%async_computation.10 | async-start | bytes 1179648 | tf_op jit(solution)/shard_map/reduce_scatter | solution.py:287
  452.3 363.5 %reduce-scatter.9.cloned.1.call-start = ((), (), s32[]{:S(2)}) async-start(), calls=%async_computation.9 | async-start | bytes 1179648 | tf_op jit(solution)/shard_map/reduce_scatter | solution.py:286
  454.1 428.8 %reduce-scatter.7.cloned.1.call-start = ((), (), s32[]{:S(2)}) async-start(), calls=%async_computation.8 | async-start | bytes 1179648 | tf_op jit(solution)/shard_map/reduce_scatter | solution.py:285
  455.9 518.4 %reduce-scatter.15.cloned.1.call-start = ((), (), s32[]{:S(2)}) async-start(), calls=%async_computation.12 | async-start | bytes 4718592 | tf_op jit(solution)/shard_map/reduce_scatter | solution.py:289
  463.8 56.9 %copy-start.6 = (bf16[1024,1024]{1,0:T(8,128)(2,1)S(1)}, bf16[1024,1024]{1,0:T(8,128)(2,1)}, u32[]{:S(2)}) copy-start(bf16[1024,1024]{1,0:T(8,128)(2,1)} %param.27) | copy-start | bytes 6291460
  463.8 56.9 %copy-start.41 = (f32[1024]{0:T(1024)S(1)}, f32[1024]{0:T(1024)}, u32[]{:S(2)}) copy-start(f32[1024]{0:T(1024)} %copy-done.40) | copy-start | bytes 12292
  463.8 56.9 %copy-start.44 = (f32[1024]{0:T(1024)S(1)}, f32[1024]{0:T(1024)}, u32[]{:S(2)}) copy-start(f32[1024]{0:T(1024)} %copy-done.43) | copy-start | bytes 12292
  463.9 56.9 %copy-start.47 = (f32[1024]{0:T(1024)S(1)}, f32[1024]{0:T(1024)}, u32[]{:S(2)}) copy-start(f32[1024]{0:T(1024)} %param.35) | copy-start | bytes 12292
  463.9 60.6 %copy-start.50 = (f32[1024]{0:T(1024)S(1)}, f32[1024]{0:T(1024)}, u32[]{:S(2)}) copy-start(f32[1024]{0:T(1024)} %get-tuple-element.286) | copy-start | bytes 12292
  463.9 60.6 %copy-start.51 = (f32[1024]{0:T(1024)S(1)}, f32[1024]{0:T(1024)}, u32[]{:S(2)}) copy-start(f32[1024]{0:T(1024)} %get-tuple-element.365) | copy-start | bytes 12292
  463.9 60.6 %copy-start.52 = (f32[1024]{0:T(1024)S(1)}, f32[1024]{0:T(1024)}, u32[]{:S(2)}) copy-start(f32[1024]{0:T(1024)} %get-tuple-element.303) | copy-start | bytes 12292
  463.9 60.6 %copy-start.53 = (f32[1024]{0:T(1024)S(1)}, f32[1024]{0:T(1024)}, u32[]{:S(2)}) copy-start(f32[1024]{0:T(1024)} %get-tuple-element.304) | copy-start | bytes 12292
  463.9 60.6 %copy-start.59 = (f32[1024]{0:T(1024)S(1)}, f32[1024]{0:T(1024)}, u32[]{:S(2)}) copy-start(f32[1024]{0:T(1024)} %get-tuple-element.382) | copy-start | bytes 12292
  566.6 407.7 %copy-start.1 = (bf16[1024,1024]{1,0:T(8,128)(2,1)S(1)}, bf16[1024,1024]{1,0:T(8,128)(2,1)}, u32[]{:S(2)}) copy-start(bf16[1024,1024]{1,0:T(8,128)(2,1)} %param.34) | copy-start | bytes 6291460
  (56 other events, 277.0 us)
Sparse Core Ops, SparseCore 0:
  66.9 88.1 all-reduce.6
  216.0 153.9 all-reduce.10
  435.1 85.5 all-reduce.8
  524.3 89.6 reduce-scatter.16
  617.8 63.8 reduce-scatter.12
  685.5 63.1 reduce-scatter.10
  752.6 63.1 reduce-scatter.8
  819.8 63.0 reduce-scatter.6
  887.1 87.2 reduce-scatter.14
where the time goes:
time: 992 us; the launch traced here: 981 us
  waiting for transfers between devices  683 us (69%)
  matrix products  101 us (10%)
  other arithmetic  68.1 us (7%)
  blocking collectives  59.1 us (6%)
  local copies, waits for them, and re-layouts  46.8 us (5%)
  between operations  15.8 us (2%)
    psum x1, waiting for transfers between devices, body(): ffn_out = lax.psum(project_t(middle, w_fc2), 'tensor') + fc2_bias  154 us
    reduce_scatter x1, waiting for transfers between devices, body(): lax.psum_scatter(grad_w_fc1, 'dp', scatter_dimension=0, tiled=True)  91.5 us
    psum x1, waiting for transfers between devices, body(): mixed = lax.psum(project_t(context, w_out), 'tensor') + out_bias  76.3 us
    reduce_scatter x1, waiting for transfers between devices, body(): lax.psum_scatter(grad_w_key, 'dp', scatter_dimension=0, tiled=True)  67.1 us
    reduce_scatter x1, waiting for transfers between devices, body(): lax.psum_scatter(grad_w_query, 'dp', scatter_dimension=0, tiled=True)  67.1 us
    reduce_scatter x1, waiting for transfers between devices, body(): lax.psum_scatter(grad_w_value, 'dp', scatter_dimension=0, tiled=True)  67 us
    reduce_scatter x1, waiting for transfers between devices, body(): lax.psum_scatter(grad_w_out, 'dp', scatter_dimension=0, tiled=True)  65.7 us
    psum x1, waiting for transfers between devices, body(): lax.psum(project_t(grad_query, w_query) + project_t(grad_key, w_key) + pr...  53.4 us
  transfers between devices with their start and end apart: 9, of which 9 were waited for; matrix products, arithmetic and copies ran while one was open for 5% of the time, Pallas kernels for 0%

commit v1 on v0

--- a/solution.py
+++ b/solution.py
@@ -180,7 +180,7 @@
     factorm = lax.rsqrt(spread + epsilon)
     normedm = centred * factorm
     middle = (normedm * mid_gain + mid_bias).astype(jnp.bfloat16)
-    ffn_out = lax.psum(project_t(middle, w_fc2), "tensor") + fc2_bias
+    ffn_out = jnp.sum(lax.all_gather(project_t(middle, w_fc2), "tensor"), axis=0) + fc2_bias
     result = stream + ffn_out
     output = result.astype(jnp.bfloat16)
     upstream = cotangent.astype(jnp.float32)

time: 992 us -> 948 us (0.956)
  waiting for transfers between devices: 683 us -> 622 us
  other arithmetic: 68.1 us -> 82.3 us
    psum x1, waiting for transfers between devices: 154 us -> 77.5 us  [body(): grad_inner = lax.psum(project_t(grad_hidden, w_fc1), 'tensor')]
    all_gather x0 -> x1, waiting for transfers between devices: none -> 58.6 us  [body(): lax.all_gather(project_t(middle, w_fc2), 'tensor')]
    reduce_scatter x1, waiting for transfers between devices: 91.5 us -> 41.3 us  [body(): lax.psum_scatter(grad_w_fc1, 'dp', scatter_dimension=0, tiled=True)]
    reduce_scatter x1, waiting for transfers between devices: 40.9 us -> 4.58 us  [body(): lax.psum_scatter(grad_w_fc2, 'dp', scatter_dimension=0, tiled=True)]
    psum x1, waiting for transfers between devices: 53.4 us -> 82.8 us  [body(): lax.psum(project_t(grad_query, w_query) + project_t(grad_key, w_key) + pr...]
    psum x1, waiting for transfers between devices: 76.3 us -> 88.1 us  [body(): mixed = lax.psum(project_t(context, w_out), 'tensor') + out_bias]
    reduce_sum x0 -> x1, other arithmetic: none -> 10.4 us  [body(): jnp.sum(lax.all_gather(project_t(middle, w_fc2), 'tensor'), axis=0)]
  transfers between devices with their start and end apart: 9 -> 10, of which waited for: 9 -> 10; matrix products, arithmetic and copies ran while one was open for 5% -> 15% of each run, Pallas kernels for 0% -> 0%
where the time goes in v1:
time: 948 us; the launch traced here: 937 us
  waiting for transfers between devices  622 us (66%)
  matrix products  102 us (11%)
  other arithmetic  82.3 us (9%)
  blocking collectives  59.2 us (6%)
  local copies, waits for them, and re-layouts  47 us (5%)
  between operations  16.1 us (2%)
    psum x1, waiting for transfers between devices, body(): mixed = lax.psum(project_t(context, w_out), 'tensor') + out_bias  88.1 us
    psum x1, waiting for transfers between devices, body(): lax.psum(project_t(grad_query, w_query) + project_t(grad_key, w_key) + pr...  82.8 us
    psum x1, waiting for transfers between devices, body(): grad_inner = lax.psum(project_t(grad_hidden, w_fc1), 'tensor')  77.5 us
    reduce_scatter x1, waiting for transfers between devices, body(): lax.psum_scatter(grad_w_out, 'dp', scatter_dimension=0, tiled=True)  67.8 us
    reduce_scatter x1, waiting for transfers between devices, body(): lax.psum_scatter(grad_w_key, 'dp', scatter_dimension=0, tiled=True)  67.1 us
    reduce_scatter x1, waiting for transfers between devices, body(): lax.psum_scatter(grad_w_value, 'dp', scatter_dimension=0, tiled=True)  67.1 us
    reduce_scatter x1, waiting for transfers between devices, body(): lax.psum_scatter(grad_w_query, 'dp', scatter_dimension=0, tiled=True)  67 us
    all_gather x1, waiting for transfers between devices, body(): lax.all_gather(project_t(middle, w_fc2), 'tensor')  58.6 us
  transfers between devices with their start and end apart: 10, of which 10 were waited for; matrix products, arithmetic and copies ran while one was open for 15% of the time, Pallas kernels for 0%

profile of v1, /device:TPU:0, one launch (start us, length us, event | category | flops | bytes accessed | tf_op | source)
XLA Modules:
  0.0 937.4 jit_solution(8013501640030070797)
XLA Ops:
  17.5 42.9 %while.47 = (s32[]{:T(128)}, f32[2,512,4,64]{1,0,3,2:T(2,128)}, f32[2,4,512]{2,1,0:T(4,128)S(1)}, s32[2]{0:T(128)S(1)}, s32[1024]{0:T(1024)S(1)}, /*index=5*/bf1...) while((s32[]{:T(128)}, f32[2,512,4,64]{1,0,3,2:T(2,128)}, ...), condition=%wide.region_5.6_spmd, body=%wide.region_2.5_spmd.sunk | while | flops 563608064 | bytes 31275212 | solution.py:77
  28.6 10.4 %dynamic_update_slice.30 = f32[2,512,4,64]{1,0,3,2:T(2,128)} dynamic-update-slice(f32[2,512,4,64]{1,0,3,2:T(2,128)} %get-tuple-element.523, f32[1,512,4,64]{1,0,3,2:T(1,128)S(1)} %copy.101, s32[]{:T(128)S(6)} %copy.108, s32[]{:T(128)} %constant.111.clone.1..sunk, s32[]{:T(128)} %constant.111.clone.1..sunk, s32[]{:T(128)} %constant.111.clone.1..sunk) | dynamic-update-slice | bytes 1048580 | tf_op jit(solution)/shard_map/while/body/eval_jaxpr/while/body/jit(dynamic_update_index_in_dim)/dynamic_update_slice | solution.py:77
  50.0 10.4 %dynamic_update_slice.30 = f32[2,512,4,64]{1,0,3,2:T(2,128)} dynamic-update-slice(f32[2,512,4,64]{1,0,3,2:T(2,128)} %get-tuple-element.523, f32[1,512,4,64]{1,0,3,2:T(1,128)S(1)} %copy.101, s32[]{:T(128)S(6)} %copy.108, s32[]{:T(128)} %constant.111.clone.1..sunk, s32[]{:T(128)} %constant.111.clone.1..sunk, s32[]{:T(128)} %constant.111.clone.1..sunk) | dynamic-update-slice | bytes 1048580 | tf_op jit(solution)/shard_map/while/body/eval_jaxpr/while/body/jit(dynamic_update_index_in_dim)/dynamic_update_slice | solution.py:77
  67.1 88.1 %all-reduce.6.cloned.1.call-done = f32[1024,1024]{1,0:T(8,128)} async-done(((f32[1024,1024]{1,0:T(8,128)}), f32[1024,1024]{1,0:T(8,128)}) %all-reduce.6.cloned.1.call-update) | async-done | bytes 4194320 | tf_op jit(solution)/shard_map/psum | solution.py:169
  185.1 7.8 fusion.67
  193.4 6.5 fusion.73
  205.8 7.2 multiply_reduce_fusion.1
  213.0 6.8 all-reduce.1
  219.9 8.2 convert_reduce_fusion.2
  232.5 8.6 convolution_bitcast_fusion
  241.4 58.6 %all-gather.3.cloned.1.call-done = f32[4096,1024]{1,0:T(8,128)} async-done(((f32[1024,1024]{1,0:T(8,128)}), f32[4096,1024]{1,0:T(8,128)}) %all-gather.3.cloned.1.call-update) | async-done | bytes 16777232 | tf_op jit(solution)/shard_map/all_gather | solution.py:183
  300.0 10.4 %reduce_sum.352 = f32[1024,1024]{1,0:T(8,128)} reduce(f32[4,1024,1024]{2,1,0:T(8,128)} %bitcast.124, f32[]{:T(128)} %constant.112.clone.1), dimensions={0}, to_apply=%region_15.16 | reduce | flops 3145728 | bytes 20971524 | tf_op jit(solution)/shard_map/reduce_sum | solution.py:183
  310.4 77.5 %all-reduce.8.cloned.1.call-done = f32[1024,1024]{1,0:T(8,128)} async-done(((f32[1024,1024]{1,0:T(8,128)}), f32[1024,1024]{1,0:T(8,128)}) %all-reduce.8.cloned.1.call-update) | async-done | bytes 4194320 | tf_op jit(solution)/shard_map/psum | solution.py:204
  387.9 8.3 fusion.59
  408.3 38.8 %while.48 = (s32[]{:T(128)}, f32[1024,4,64]{0,2,1:T(8,128)S(1)}, f32[1024,4,64]{0,2,1:T(8,128)}, bf16[2,512,4,64]{1,3,2,0:T(8,128)(2,1)S(1)}, s32[2]{0:T(128)S(1...) while((s32[]{:T(128)}, f32[1024,4,64]{0,2,1:T(8,128)S(1)}, ...), condition=%wide.region_27.28_spmd.clone, body=%wide.region_25.27_spmd.clone.sunk | while | flops 1376647680 | bytes 80812376 | solution.py:120
  454.9 6.9 fusion.68
  484.8 82.8 %all-reduce.10.cloned.1.call-done = f32[1024,1024]{1,0:T(8,128)} async-done(((f32[1024,1024]{1,0:T(8,128)}), f32[1024,1024]{1,0:T(8,128)}) %all-reduce.10.cloned.1.call-update) | async-done | bytes 4194320 | tf_op jit(solution)/shard_map/psum | solution.py:227
  571.3 40.7 %all-reduce = (f32[1024]{0:T(1024)}, f32[1024]{0:T(1024)}, f32[1024]{0:T(1024)}, f32[1024]{0:T(1024)}, f32[1024]{0:T(1024)}, /*index=5*/f32[1024]{0:T(1024)}, f3...) all-reduce(f32[1024]{0:T(1024)S(1)} %get-tuple-element.292, ...), channel_id=1, replica_groups=mesh['dp'=8,'tensor'=4] {'dp'}, use_global_device_ids=true, to_apply=%region_38.39 | all-reduce | flops 11784 | bytes 94272 | tf_op jit(solution)/shard_map/psum | solution.py:262
  613.2 6.5 fusion.48
  619.7 41.3 %reduce-scatter.15.cloned.1.call-done = f32[128,1024]{1,0:T(8,128)} async-done(((f32[1024,1024]{1,0:T(8,128)}), f32[128,1024]{1,0:T(8,128)}) %reduce-scatter.15.cloned.1.call-update) | async-done | bytes 524304 | tf_op jit(solution)/shard_map/reduce_scatter | solution.py:289
  661.0 67.8 %reduce-scatter.13.cloned.1.call-done = f32[128,256]{1,0:T(8,128)} async-done(((f32[1024,256]{1,0:T(8,128)}), f32[128,256]{1,0:T(8,128)}) %reduce-scatter.13.cloned.1.call-update) | async-done | bytes 131088 | tf_op jit(solution)/shard_map/reduce_scatter | solution.py:288
  728.8 67.1 %reduce-scatter.11.cloned.1.call-done = f32[128,256]{1,0:T(8,128)} async-done(((f32[1024,256]{1,0:T(8,128)}), f32[128,256]{1,0:T(8,128)}) %reduce-scatter.11.cloned.1.call-update) | async-done | bytes 131088 | tf_op jit(solution)/shard_map/reduce_scatter | solution.py:287
  796.0 67.1 %reduce-scatter.9.cloned.1.call-done = f32[128,256]{1,0:T(8,128)} async-done(((f32[1024,256]{1,0:T(8,128)}), f32[128,256]{1,0:T(8,128)}) %reduce-scatter.9.cloned.1.call-update) | async-done | bytes 131088 | tf_op jit(solution)/shard_map/reduce_scatter | solution.py:286
  863.1 67.0 %reduce-scatter.7.cloned.1.call-done = f32[128,256]{1,0:T(8,128)} async-done(((f32[1024,256]{1,0:T(8,128)}), f32[128,256]{1,0:T(8,128)}) %reduce-scatter.7.cloned.1.call-update) | async-done | bytes 131088 | tf_op jit(solution)/shard_map/reduce_scatter | solution.py:285
  (263 shorter events, 158.1 us)
Async XLA Ops:
  7.2 177.9 %copy-start = (bf16[1024,1024]{1,0:T(8,128)(2,1)S(1)}, bf16[1024,1024]{1,0:T(8,128)(2,1)}, u32[]{:S(2)}) copy-start(bf16[1024,1024]{1,0:T(8,128)(2,1)} %param.34) | copy-start | bytes 6291460
  7.2 147.9 %all-reduce.6.cloned.1.call-start = ((), (), s32[]{:S(2)}) async-start(), calls=%async_computation.6 | async-start | bytes 8388608 | tf_op jit(solution)/shard_map/psum | solution.py:169
  8.2 53.6 %copy-start.52 = (f32[256]{0:T(256)}, f32[256]{0:T(256)S(1)}, u32[]{:S(2)}) copy-start(f32[256]{0:T(256)S(1)} %mul.324) | copy-start | bytes 3076
  62.8 92.3 %copy-start.40 = (f32[1024]{0:T(1024)S(1)}, f32[1024]{0:T(1024)}, u32[]{:S(2)}) copy-start(f32[1024]{0:T(1024)} %param.45) | copy-start | bytes 12292
  66.8 92.5 %copy-start.46 = (f32[1024]{0:T(1024)S(1)}, f32[1024]{0:T(1024)}, u32[]{:S(2)}) copy-start(f32[1024]{0:T(1024)} %param.37) | copy-start | bytes 12292
  66.8 92.5 %copy-start.50 = (f32[1024]{0:T(1024)S(1)}, f32[1024]{0:T(1024)}, u32[]{:S(2)}) copy-start(f32[1024]{0:T(1024)} %param.38) | copy-start | bytes 12292
  66.8 233.2 %all-gather.3.cloned.1.call-start = ((), (), s32[]{:S(2)}) async-start(), calls=%async_computation.15 | async-start | bytes 20971520 | tf_op jit(solution)/shard_map/all_gather | solution.py:183
  193.0 194.9 %all-reduce.8.cloned.1.call-start = ((), (), s32[]{:S(2)}) async-start(), calls=%async_computation.7 | async-start | bytes 8388608 | tf_op jit(solution)/shard_map/psum | solution.py:204
  232.4 247.8 %reduce-scatter.17.cloned.1.call-start = ((), (), s32[]{:S(2)}) async-start(), calls=%async_computation.14 | async-start | bytes 4718592 | tf_op jit(solution)/shard_map/reduce_scatter | solution.py:290
  241.2 326.4 %all-reduce.10.cloned.1.call-start = ((), (), s32[]{:S(2)}) async-start(), calls=%async_computation.8 | async-start | bytes 8388608 | tf_op jit(solution)/shard_map/psum | solution.py:227
  300.0 87.9 %copy-start.54 = (f32[1024]{0:T(1024)S(1)}, f32[1024]{0:T(1024)}, u32[]{:S(2)}) copy-start(f32[1024]{0:T(1024)} %param.47) | copy-start | bytes 12292
  453.4 207.6 %reduce-scatter.15.cloned.1.call-start = ((), (), s32[]{:S(2)}) async-start(), calls=%async_computation.13 | async-start | bytes 4718592 | tf_op jit(solution)/shard_map/reduce_scatter | solution.py:289
  461.8 267.0 %reduce-scatter.13.cloned.1.call-start = ((), (), s32[]{:S(2)}) async-start(), calls=%async_computation.12 | async-start | bytes 1179648 | tf_op jit(solution)/shard_map/reduce_scatter | solution.py:288
  466.5 329.5 %reduce-scatter.11.cloned.1.call-start = ((), (), s32[]{:S(2)}) async-start(), calls=%async_computation.11 | async-start | bytes 1179648 | tf_op jit(solution)/shard_map/reduce_scatter | solution.py:287
  469.5 393.6 %reduce-scatter.9.cloned.1.call-start = ((), (), s32[]{:S(2)}) async-start(), calls=%async_computation.10 | async-start | bytes 1179648 | tf_op jit(solution)/shard_map/reduce_scatter | solution.py:286
  471.3 96.2 %copy-start.6 = (bf16[1024,1024]{1,0:T(8,128)(2,1)S(1)}, bf16[1024,1024]{1,0:T(8,128)(2,1)}, u32[]{:S(2)}) copy-start(bf16[1024,1024]{1,0:T(8,128)(2,1)} %param.27) | copy-start | bytes 6291460
  471.4 96.2 %copy-start.39 = (f32[1024]{0:T(1024)S(1)}, f32[1024]{0:T(1024)}, u32[]{:S(2)}) copy-start(f32[1024]{0:T(1024)} %copy-done.38) | copy-start | bytes 12292
  471.4 96.2 %copy-start.42 = (f32[1024]{0:T(1024)S(1)}, f32[1024]{0:T(1024)}, u32[]{:S(2)}) copy-start(f32[1024]{0:T(1024)} %copy-done.41) | copy-start | bytes 12292
  471.4 96.2 %copy-start.45 = (f32[1024]{0:T(1024)S(1)}, f32[1024]{0:T(1024)}, u32[]{:S(2)}) copy-start(f32[1024]{0:T(1024)} %param.35) | copy-start | bytes 12292
  471.4 458.7 %reduce-scatter.7.cloned.1.call-start = ((), (), s32[]{:S(2)}) async-start(), calls=%async_computation.9 | async-start | bytes 1179648 | tf_op jit(solution)/shard_map/reduce_scatter | solution.py:285
  475.0 96.3 %copy-start.48 = (f32[1024]{0:T(1024)S(1)}, f32[1024]{0:T(1024)}, u32[]{:S(2)}) copy-start(f32[1024]{0:T(1024)} %get-tuple-element.286) | copy-start | bytes 12292
  475.0 96.3 %copy-start.49 = (f32[1024]{0:T(1024)S(1)}, f32[1024]{0:T(1024)}, u32[]{:S(2)}) copy-start(f32[1024]{0:T(1024)} %get-tuple-element.363) | copy-start | bytes 12292
  475.0 96.3 %copy-start.55 = (f32[1024]{0:T(1024)S(1)}, f32[1024]{0:T(1024)}, u32[]{:S(2)}) copy-start(f32[1024]{0:T(1024)} %get-tuple-element.380) | copy-start | bytes 12292
  613.2 316.9 %copy-start.1 = (bf16[1024,1024]{1,0:T(8,128)(2,1)S(1)}, bf16[1024,1024]{1,0:T(8,128)(2,1)}, u32[]{:S(2)}) copy-start(bf16[1024,1024]{1,0:T(8,128)(2,1)} %param.34) | copy-start | bytes 6291460
  (53 other events, 216.6 us)
Sparse Core Ops, SparseCore 0:
  66.9 88.1 all-reduce.5
  193.1 106.8 all-gather.2
  302.4 85.4 all-reduce.7
  391.4 88.8 reduce-scatter.16
  482.4 85.1 all-reduce.9
  571.6 89.3 reduce-scatter.14
  665.0 63.8 reduce-scatter.12
  732.8 63.1 reduce-scatter.10
  800.0 63.1 reduce-scatter.8
  866.9 63.1 reduce-scatter.6
